TPU v7x, 32 devices: a whole 2x2x4 slice. The times are simulated.
32 devices in a mesh: parts: 2 (over y), row: 4 (over x, core), col: 4 (over z).
Axes of the slice: x: 2, y: 2, z: 4, core: 2. Of those that a mesh axis runs over, the one named last changes fastest.
Arguments:
- latent: bfloat16 [4, 32, 32, 640], P('parts', 'row', 'col'), parts along dimension 0, may hold values from -6 to 6
- timestep: int32 [4], P('parts'), parts along dimension 0, may hold values from 0 to 999
- gn_gain: float32 [640], replicated, may hold values from 0.25 to 1.75
- gn_bias: float32 [640], replicated, may hold values from -3 to 3
- conv_weight: bfloat16 [3, 3, 640, 640], P(None, None, None, 'row'), may hold values from -0.078125 to 0.078125
- conv_bias: float32 [640], replicated, may hold values from -3 to 3
- time_weight: bfloat16 [320, 640], replicated, may hold values from -0.625 to 0.625
- ln_gain: float32 [640], replicated, may hold values from 0.25 to 1.75
- q_weight: bfloat16 [640, 384], replicated, may hold values from -0.5 to 0.5
- k_weight: bfloat16 [640, 384], replicated, may hold values from -0.25 to 0.25
- v_weight: bfloat16 [640, 384], replicated, may hold values from -0.25 to 0.25
- out_weight: bfloat16 [384, 640], replicated, may hold values from -0.3125 to 0.3125
- stale_keys: bfloat16 [4, 32, 32, 384], P('parts', 'row', 'col'), parts along dimension 0, may hold values from -40 to 40
- stale_values: bfloat16 [4, 32, 32, 384], P('parts', 'row', 'col'), parts along dimension 0, may hold values from -6 to 6
Outputs:
- mixed: bfloat16 [4, 32, 32, 640], P('parts', 'row', 'col'), parts along dimension 0
- fresh_keys: bfloat16 [4, 32, 32, 384], P('parts', 'row', 'col'), parts along dimension 0
- fresh_values: bfloat16 [4, 32, 32, 384], P('parts', 'row', 'col'), parts along dimension 0
There are 2 independent parts, one for each index of `parts`. A program takes and returns all parts, laid end to end along the dimension named above; an argument that names none is the same for every part. Nothing has to cross between parts.
All inputs are finite; a program needn't handle non-finite values.
Results may differ from a plain program's by a relative error of at most 0.012.
Values may be sent and summed in bfloat16 or wider, within the bound.
A program may use at most 64 MiB of HBM per device.

v0:
```python
import jax
import jax.numpy as jnp
from jax import lax
from jax.sharding import PartitionSpec as P

HD = 64
GROUPS = 32


def with_halo(cells, sides, width):
    for axis, dim in sides:
        count = lax.axis_size(axis)
        ends = count - 1
        head = lax.slice_in_dim(cells, 0, width, axis=dim)
        tail = lax.slice_in_dim(cells, cells.shape[dim] - width, cells.shape[dim], axis=dim)
        cells = jnp.concatenate(
            [
                lax.ppermute(tail, axis, [(i, (i + 1) % count) for i in range(ends)]),
                cells,
                lax.ppermute(head, axis, [((i + 1) % count, i) for i in range(ends)]),
            ],
            axis=dim,
        )
    return cells


def time_features(timestep, width):
    half = width // 2
    freqs = jnp.exp(-jnp.log(10000.0) * jnp.arange(half, dtype=jnp.float32) / half)
    angles = timestep.astype(jnp.float32)[:, None] * freqs[None, :]
    return jnp.concatenate([jnp.cos(angles), jnp.sin(angles)], axis=1)


def make_fold(query_all, own_query, own_key, span, heads):
    batch, rows_q, inner = query_all.shape
    head_size = inner // heads
    query_heads = query_all.reshape(batch, rows_q, heads, head_size)
    query_block = jnp.arange(rows_q, dtype=jnp.int32) // span

    def fold(carry, pieces, start):
        keys_piece, values_piece = pieces
        count = keys_piece.shape[1]
        width = 128
        keys_blocks = keys_piece.reshape(batch, count // width, width, heads, head_size).transpose(
            1, 0, 2, 3, 4
        )
        values_blocks = values_piece.reshape(
            batch, count // width, width, heads, head_size
        ).transpose(1, 0, 2, 3, 4)
        offsets = width * jnp.arange(count // width, dtype=jnp.int32)

        def step(state, items):
            peak, total, summed = state
            keys_block, values_block, offset = items
            scores = jnp.einsum(
                "bqhd,bkhd->bhqk", query_heads, keys_block, preferred_element_type=jnp.float32
            )
            key_block = (offset + jnp.arange(width, dtype=jnp.int32)) // span
            masked = (query_block == own_query)[:, None] & (key_block == own_key)[None, :]
            scores = jnp.where(masked, -1e30, scores)
            new_peak = jnp.maximum(peak, jnp.max(scores, axis=-1))
            weights = jnp.where(masked, 0.0, jnp.exp(scores - new_peak[..., None]))
            factor = jnp.exp(peak - new_peak)
            total = total * factor + jnp.sum(weights, axis=-1)
            summed = summed * factor[..., None] + jnp.einsum(
                "bhqk,bkhd->bhqd",
                weights.astype(jnp.bfloat16),
                values_block,
                preferred_element_type=jnp.float32,
            )
            return ((new_peak, total, summed), None)

        result, unused = lax.scan(step, carry, (keys_blocks, values_blocks, offsets))
        return result

    return fold


def body(
    latent,
    timestep,
    gn_gain,
    gn_bias,
    conv_weight,
    conv_bias,
    time_weight,
    ln_gain,
    q_weight,
    k_weight,
    v_weight,
    out_weight,
    stale_keys,
    stale_values,
):
    batch, rows, columns, channels = latent.shape
    inner = q_weight.shape[1]
    heads = inner // HD
    span = rows * columns
    count_all = span * lax.axis_size("row") * lax.axis_size("col") * (channels // GROUPS)
    emb = jax.nn.silu(time_features(timestep, time_weight.shape[0])).astype(jnp.bfloat16)
    temb = jnp.dot(emb, time_weight, preferred_element_type=jnp.float32)
    values = latent.astype(jnp.float32)
    grouped = values.reshape(batch, span, GROUPS, channels // GROUPS)
    sum_one = jnp.sum(grouped, axis=(1, 3))
    sum_two = jnp.sum(grouped * grouped, axis=(1, 3))
    total_one, total_two = lax.psum((sum_one, sum_two), ("row", "col"))
    mean = total_one / count_all
    var = total_two / count_all - mean * mean
    normed = (grouped - mean[:, None, :, None]) * lax.rsqrt(var + 1e-05)[:, None, :, None]
    normed = normed.reshape(batch, rows, columns, channels) * gn_gain + gn_bias
    act = jax.nn.silu(normed).astype(jnp.bfloat16)
    padded = with_halo(act, (("row", 1), ("col", 2)), 1)
    piece = lax.all_gather(conv_weight, "row", axis=3, tiled=True)
    result = jnp.zeros((batch, rows, columns, piece.shape[3]), jnp.float32)
    for down in range(3):
        for across in range(3):
            result = result + jnp.dot(
                padded[:, down : down + rows, across : across + columns, :],
                piece[down, across],
                preferred_element_type=jnp.float32,
            )
    hidden = (values + result + conv_bias + temb[:, None, None, :]).astype(jnp.bfloat16)
    hidden_f = hidden.astype(jnp.float32)
    centre = hidden_f - jnp.mean(hidden_f, axis=-1, keepdims=True)
    spread = jnp.mean(centre * centre, axis=-1, keepdims=True)
    layer_normed = (centre * lax.rsqrt(spread + 1e-05) * ln_gain).astype(jnp.bfloat16)
    queries = (
        jnp.dot(layer_normed, q_weight, preferred_element_type=jnp.float32)
        * (1.0 / jnp.sqrt(jnp.float32(HD)))
    ).astype(jnp.bfloat16)
    fresh_keys = jnp.dot(layer_normed, k_weight, preferred_element_type=jnp.float32).astype(
        jnp.bfloat16
    )
    fresh_values = jnp.dot(layer_normed, v_weight, preferred_element_type=jnp.float32).astype(
        jnp.bfloat16
    )
    query_rows = queries.reshape(batch, span, inner)
    stale_k = stale_keys.reshape(batch, span, inner)
    stale_v = stale_values.reshape(batch, span, inner)
    own_q = query_rows.reshape(batch, span, heads, HD)
    own_k = fresh_keys.reshape(batch, span, heads, HD)
    own_v = fresh_values.reshape(batch, span, heads, HD)
    own_scores = jnp.einsum("bqhd,bkhd->bhqk", own_q, own_k, preferred_element_type=jnp.float32)
    own_peak = jnp.max(own_scores, axis=-1)
    query_all = lax.all_gather(query_rows, "col", axis=1, tiled=True)
    query_index = lax.axis_index("col")
    key_index = lax.axis_index("row")
    rows_q = query_all.shape[1]
    initial = (
        jnp.full((batch, heads, rows_q), -1e30, jnp.float32),
        jnp.zeros((batch, heads, rows_q), jnp.float32),
        jnp.zeros((batch, heads, rows_q, HD), jnp.float32),
    )
    fold = make_fold(query_all, query_index, key_index, span, heads)
    peak, total, summed = fold(
        initial,
        (
            lax.all_gather(stale_k, "row", axis=1, tiled=True),
            lax.all_gather(stale_v, "row", axis=1, tiled=True),
        ),
        jnp.int32(0),
    )
    mine = lax.dynamic_slice_in_dim(peak, query_index * span, span, 2)
    raised = lax.dynamic_update_slice_in_dim(
        peak, jnp.maximum(mine, own_peak), query_index * span, 2
    )
    top = lax.pmax(raised.astype(jnp.bfloat16), "col").astype(raised.dtype)
    factor = jnp.exp(peak - top)
    scaled_sum = summed * factor[..., None]
    scaled_total = total * factor
    part_sum, part_total = (
        lax.psum_scatter(
            scaled_sum.astype(jnp.bfloat16), "col", scatter_dimension=2, tiled=True
        ).astype(jnp.float32),
        lax.psum_scatter(
            scaled_total.astype(jnp.bfloat16), "col", scatter_dimension=2, tiled=True
        ).astype(jnp.float32),
    )
    top_own = lax.dynamic_slice_in_dim(top, query_index * span, span, 2)
    own_weights = jnp.exp(own_scores - top_own[..., None])
    part_total = part_total + jnp.sum(own_weights, axis=-1)
    part_sum = part_sum + jnp.einsum(
        "bhqk,bkhd->bhqd",
        own_weights.astype(jnp.bfloat16),
        own_v,
        preferred_element_type=jnp.float32,
    )
    attn = (
        (part_sum / part_total[..., None])
        .transpose(0, 2, 1, 3)
        .reshape(batch, span, inner)
        .astype(jnp.bfloat16)
    )
    mixed = hidden_f.reshape(batch, span, channels) + jnp.dot(
        attn, out_weight, preferred_element_type=jnp.float32
    )
    mixed = mixed.astype(jnp.bfloat16).reshape(batch, rows, columns, channels)
    return (mixed, fresh_keys, fresh_values)


def solution(mesh):
    placed = (
        P("parts", "row", "col", None),
        P("parts"),
        P(),
        P(),
        P(None, None, None, "row"),
        P(),
        P(),
        P(),
        P(),
        P(),
        P(),
        P(),
        P("parts", "row", "col", None),
        P("parts", "row", "col", None),
    )
    return jax.shard_map(
        body,
        mesh=mesh,
        in_specs=placed,
        out_specs=(
            P("parts", "row", "col", None),
            P("parts", "row", "col", None),
            P("parts", "row", "col", None),
        ),
        check_vma=False,
    )
```

profile of v0, /device:TPU:0, one launch (start us, length us, event | category | flops | bytes accessed | tf_op | source)
XLA Modules:
  0.0 180.5 jit_solution(7372070736849188195)
XLA Ops:
  8.6 35.7 %all-reduce = (f32[2,32]{1,0:T(2,128)S(1)}, f32[2,32]{1,0:T(2,128)S(1)}) all-reduce(f32[2,32]{1,0:T(2,128)S(1)} %reduce_sum.76, f32[2,32]{1,0:T(2,128)S(1)} %reduce_sum.73), channel_id=1, replica_groups=mesh['parts'=2,'row'=4,'col'=4] {'row','col'}, use_global_device_ids=true, to_apply=%region_5.6 | all-reduce | flops 128 | bytes 1024 | tf_op jit(solution)/shard_map/psum | solution.py:106
  46.2 1.3 collective-permute-start.1
  47.8 10.8 %all_gather.13 = bf16[2,256,384]{2,0,1:T(2,128)(2,1)S(1)} all-gather(bf16[2,64,384]{2,0,1:T(2,128)(2,1)S(1)} %bitcast.148), channel_id=1, replica_groups=mesh['parts'=2,'row'=4,'col'=4] {'row'}, dimensions={1}, use_global_device_ids=true | all-gather | bytes 491520 | tf_op jit(solution)/shard_map/all_gather | solution.py:158
  58.9 9.1 %all_gather.15 = bf16[2,256,384]{2,0,1:T(2,128)(2,1)S(1)} all-gather(bf16[2,64,384]{2,0,1:T(2,128)(2,1)S(1)} %bitcast.147), channel_id=1, replica_groups=mesh['parts'=2,'row'=4,'col'=4] {'row'}, dimensions={1}, use_global_device_ids=true | all-gather | bytes 491520 | tf_op jit(solution)/shard_map/all_gather | solution.py:159
  68.0 1.3 collective-permute-start.2
  69.3 1.3 collective-permute-start.3
  73.5 1.8 %collective-permute-done.3 = bf16[2,10,1,640]{3,2,1,0:T(2,128)(2,1)S(1)} collective-permute-done((bf16[2,10,1,640]{3,2,1,0:T(2,128)(2,1)S(1)}, bf16[2,10,1,640]{3,2,1,0:T(2,128)(2,1)S(1)}, u32[]{:S(2)}, u32[]{:S(2)}) %collective-permute-start.3) | collective-permute-done | bytes 25632 | tf_op jit(solution)/shard_map/ppermute | solution.py:20
  75.6 1.5 fusion.41
  77.1 1.5 fusion.38
  78.6 1.5 fusion.39
  80.1 1.5 fusion.37
  81.6 1.5 fusion.40
  83.1 1.5 fusion.35
  84.7 1.5 fusion.36
  86.2 1.5 fusion.21
  87.7 1.7 fusion.86
  93.7 15.4 %all_gather.14 = bf16[2,256,384]{2,1,0:T(8,128)(2,1)S(1)} all-gather(bf16[2,64,384]{2,1,0:T(8,128)(2,1)S(1)} %bitcast.145), channel_id=1, replica_groups=mesh['parts'=2,'row'=4,'col'=4] {'col'}, dimensions={1}, use_global_device_ids=true | all-gather | bytes 491520 | tf_op jit(solution)/shard_map/all_gather | solution.py:145
  109.3 8.7 %while.17 = (s32[]{:T(128)}, f32[2,6,256]{2,1,0:T(8,128)S(1)}, f32[2,6,256]{2,1,0:T(8,128)S(1)}, f32[2,6,256,64]{2,3,1,0:T(8,128)S(1)}, s32[]{:T(128)}, /*index=...) while((s32[]{:T(128)}, f32[2,6,256]{2,1,0:T(8,128)S(1)}, ...), condition=%wide.region_11.12_spmd.clone, body=%wide.region_8.11_spmd.clone.sunk | while | flops 104451456 | bytes 8988089 | solution.py:73
  110.7 1.4 fusion.108
  115.0 1.4 fusion.108
  119.5 8.7 %pmax.7 = bf16[2,6,256]{2,1,0:T(8,128)(2,1)S(1)} all-reduce(bf16[2,6,256]{2,1,0:T(8,128)(2,1)S(1)} %convert_element_type.78), channel_id=1, replica_groups=mesh['parts'=2,'row'=4,'col'=4] {'col'}, use_global_device_ids=true, to_apply=%region_13.14 | all-reduce | flops 3072 | bytes 12288 | tf_op jit(solution)/shard_map/pmax | solution.py:167
  129.8 1.4 multiply_convert_fusion
  131.8 15.8 %reduce-scatter.7.cloned.1.call-done = bf16[64,12]{1,0:T(8,128)(2,1)} async-done(((bf16[256,12]{1,0:T(8,128)(2,1)}), bf16[64,12]{1,0:T(8,128)(2,1)}) %reduce-scatter.7.cloned.1.call-update) | async-done | bytes 1552
  148.5 23.0 %reduce-scatter.5.cloned.1.call-done = bf16[2,6,64,64]{3,2,1,0:T(8,128)(2,1)} async-done(((bf16[2,6,256,64]{3,2,1,0:T(8,128)(2,1)}), bf16[2,6,64,64]{3,2,1,0:T(8,128)(2,1)}) %reduce-scatter.5.cloned.1.call-update) | async-done | bytes 98320 | tf_op jit(solution)/shard_map/reduce_scatter | solution.py:172
  (125 shorter events, 24.0 us)
Async XLA Ops:
  7.2 165.9 %copy-start = (bf16[384,640]{1,0:T(8,128)(2,1)S(1)}, bf16[384,640]{1,0:T(8,128)(2,1)}, u32[]{:S(2)}) copy-start(bf16[384,640]{1,0:T(8,128)(2,1)} %param.27) | copy-start | bytes 1474564
  7.2 1.0 copy-start.4
  7.2 37.6 %copy-start.13 = (f32[640]{0:T(1024)S(1)}, f32[640]{0:T(1024)}, u32[]{:S(2)}) copy-start(f32[640]{0:T(1024)} %param.18) | copy-start | bytes 7684
  7.2 37.6 %copy-start.12 = (f32[640]{0:T(1024)S(1)}, f32[640]{0:T(1024)}, u32[]{:S(2)}) copy-start(f32[640]{0:T(1024)} %param.19) | copy-start | bytes 7684
  7.2 40.3 %copy-start.16 = (s32[2]{0:T(128)S(1)}, s32[2]{0:T(128)}, u32[]{:S(2)}) copy-start(s32[2]{0:T(128)} %param.17) | copy-start | bytes 28
  7.2 40.3 %copy-start.10 = (bf16[2,8,8,384]{3,2,1,0:T(8,128)(2,1)S(1)}, bf16[2,8,8,384]{3,2,1,0:T(8,128)(2,1)}, u32[]{:S(2)}) copy-start(bf16[2,8,8,384]{3,2,1,0:T(8,128)(2,1)} %param.28) | copy-start | bytes 294916
  7.2 40.4 %copy-start.11 = (bf16[2,8,8,384]{3,2,1,0:T(8,128)(2,1)S(1)}, bf16[2,8,8,384]{3,2,1,0:T(8,128)(2,1)}, u32[]{:S(2)}) copy-start(bf16[2,8,8,384]{3,2,1,0:T(8,128)(2,1)} %param.29) | copy-start | bytes 294916
  7.2 51.4 %copy-start.7 = (bf16[320,640]{1,0:T(8,128)(2,1)S(1)}, bf16[320,640]{1,0:T(8,128)(2,1)}, u32[]{:S(2)}) copy-start(bf16[320,640]{1,0:T(8,128)(2,1)} %param.22) | copy-start | bytes 1228804
  7.3 68.3 %all-gather.2.cloned.1.call-start = ((), (), s32[]{:S(2)}) async-start(), calls=%async_computation.2 | async-start | bytes 9216000 | tf_op jit(solution)/shard_map/all_gather | solution.py:113
  8.0 139.6 %reduce-scatter.7.cloned.1.call-start = ((), (), s32[]{:S(2)}) async-start(), calls=%async_computation.4 | async-start | bytes 81920
  44.9 23.0 %collective-permute-start = (bf16[2,1,8,640]{3,2,1,0:T(8,128)(2,1)S(1)}, bf16[2,1,8,640]{3,2,1,0:T(8,128)(2,1)S(1)}, u32[]{:S(2)}, u32[]{:S(2)}) collective-permute-start(bf16[2,1,8,640]{3,2,1,0:T(8,128)(2,1)S(1)} %get-tuple-element.235), channel_id=1, source_target_pairs={{0,4},{4,8},{8,12},{1,5},{5,9},{9,13},{2,6},{6,10},{10,14},{3,7},{... | collective-permute-start | bytes 61448 | tf_op jit(solution)/shard_map/ppermute | solution.py:18
  46.2 21.7 %collective-permute-start.1 = (bf16[2,1,8,640]{3,2,1,0:T(8,128)(2,1)S(1)}, bf16[2,1,8,640]{3,2,1,0:T(8,128)(2,1)S(1)}, u32[]{:S(2)}, u32[]{:S(2)}) collective-permute-start(bf16[2,1,8,640]{3,2,1,0:T(8,128)(2,1)S(1)} %get-tuple-element.236), channel_id=1, source_target_pairs={{4,0},{8,4},{12,8},{5,1},{9,5},{13,9},{6,2},{10,6},{14,10},{7,3},{... | collective-permute-start | bytes 61448 | tf_op jit(solution)/shard_map/ppermute | solution.py:20
  68.0 5.5 %collective-permute-start.2 = (bf16[2,10,1,640]{3,2,1,0:T(2,128)(2,1)S(1)}, bf16[2,10,1,640]{3,2,1,0:T(2,128)(2,1)S(1)}, u32[]{:S(2)}, u32[]{:S(2)}) collective-permute-start(bf16[2,10,1,640]{3,2,1,0:T(2,128)(2,1)S(1)} %get-tuple-element.233), channel_id=1, source_target_pairs={{0,1},{1,2},{2,3},{4,5},{5,6},{6,7},{8,9},{9,10},{10,11},{12,13},{... | collective-permute-start | bytes 76808 | tf_op jit(solution)/shard_map/ppermute | solution.py:18
  69.3 6.0 %collective-permute-start.3 = (bf16[2,10,1,640]{3,2,1,0:T(2,128)(2,1)S(1)}, bf16[2,10,1,640]{3,2,1,0:T(2,128)(2,1)S(1)}, u32[]{:S(2)}, u32[]{:S(2)}) collective-permute-start(bf16[2,10,1,640]{3,2,1,0:T(2,128)(2,1)S(1)} %get-tuple-element.234), channel_id=1, source_target_pairs={{1,0},{2,1},{3,2},{5,4},{6,5},{7,6},{9,8},{10,9},{11,10},{13,12},{... | collective-permute-start | bytes 76808 | tf_op jit(solution)/shard_map/ppermute | solution.py:20
  86.2 1.5 copy-start.14
  87.7 1.9 %copy-start.15 = (f32[640]{0:T(1024)S(1)}, f32[640]{0:T(1024)}, u32[]{:S(2)}) copy-start(f32[640]{0:T(1024)} %param.23) | copy-start | bytes 7684
  87.7 2.0 %copy-start.5 = (bf16[640,384]{1,0:T(8,128)(2,1)S(1)}, bf16[640,384]{1,0:T(8,128)(2,1)}, u32[]{:S(2)}) copy-start(bf16[640,384]{1,0:T(8,128)(2,1)} %param.25) | copy-start | bytes 1474564
  89.4 19.7 %copy-start.1 = (f32[2,8,8,640]{3,2,1,0:T(8,128)}, f32[2,8,8,640]{3,2,1,0:T(8,128)S(1)}, u32[]{:S(2)}) copy-start(f32[2,8,8,640]{3,2,1,0:T(8,128)S(1)} %get-tuple-element.242) | copy-start | bytes 983044
  112.1 1.0 copy-start.3
  116.4 1.0 copy-start.3
  129.2 42.2 %reduce-scatter.5.cloned.1.call-start = ((), (), s32[]{:S(2)}) async-start(), calls=%async_computation.3 | async-start | bytes 983040 | tf_op jit(solution)/shard_map/reduce_scatter | solution.py:172
  129.7 1.4 copy-start.6
  131.4 41.4 %copy-start.9 = (bf16[2,8,8,384]{3,2,1,0:T(8,128)(2,1)}, bf16[2,8,8,384]{3,2,1,0:T(8,128)(2,1)S(1)}, u32[]{:S(2)}) copy-start(bf16[2,8,8,384]{3,2,1,0:T(8,128)(2,1)S(1)} %convolution_convert_fusion) | copy-start | bytes 294916
  131.8 41.3 %copy-start.2 = (f32[2,8,8,640]{3,2,1,0:T(8,128)S(1)}, f32[2,8,8,640]{3,2,1,0:T(8,128)}, u32[]{:S(2)}) copy-start(f32[2,8,8,640]{3,2,1,0:T(8,128)} %copy-done.1) | copy-start | bytes 983044
  (1 other events, 0.6 us)
Sparse Core Ops, SparseCore 0:
  9.6 59.9 all-gather.1
  129.3 18.1 reduce-scatter.6
  150.0 21.4 reduce-scatter.4
where the time goes:
time: 181 us
  blocking collectives  79.7 us (44%)
  waiting for transfers between devices  41.3 us (23%)
  matrix products  22.8 us (13%)
  between operations  14.4 us (8%)
  local copies, waits for them, and re-layouts  12 us (7%)
  starting transfers between devices  5.28 us (3%)
  other arithmetic  4.77 us (3%)
    psum x1, blocking collectives, body(): total_one, total_two = lax.psum((sum_one, sum_two), ('row', 'col'))  35.7 us
    reduce_scatter x1, waiting for transfers between devices, body(): lax.psum_scatter(scaled_sum.astype(jnp.bfloat16), 'col', scatter_dimensio...  23 us
    unnamed x4, waiting for transfers between devices  16.5 us
    all_gather x1, blocking collectives, body(): query_all = lax.all_gather(query_rows, 'col', axis=1, tiled=True)  15.4 us
    dot_general x9, matrix products, body(): jnp.dot(padded[:, down:down + rows, across:across + columns, :], piece[do...  13.7 us
    all_gather x1, blocking collectives, body(): lax.all_gather(stale_k, 'row', axis=1, tiled=True)  10.8 us
    all_gather x1, blocking collectives, body(): lax.all_gather(stale_v, 'row', axis=1, tiled=True)  9.07 us
    pmax x1, blocking collectives, body(): top = lax.pmax(raised.astype(jnp.bfloat16), 'col').astype(raised.dtype)  8.73 us
  transfers between devices with their start and end apart: 7, of which 3 were waited for; matrix products, arithmetic and copies ran while one was open for 4% of the time, Pallas kernels for 0%

commit v1 on v0

--- a/solution.py
+++ b/solution.py
@@ -103,7 +103,7 @@
     grouped = values.reshape(batch, span, GROUPS, channels // GROUPS)
     sum_one = jnp.sum(grouped, axis=(1, 3))
     sum_two = jnp.sum(grouped * grouped, axis=(1, 3))
-    total_one, total_two = lax.psum((sum_one, sum_two), ("row", "col"))
+    total_one, total_two = lax.psum(lax.psum((sum_one, sum_two), "col"), "row")
     mean = total_one / count_all
     var = total_two / count_all - mean * mean
     normed = (grouped - mean[:, None, :, None]) * lax.rsqrt(var + 1e-05)[:, None, :, None]

time: 181 us -> 177 us (0.978)
  blocking collectives: 79.7 us -> 67.6 us
  waiting for transfers between devices: 41.3 us -> 48.7 us
    psum x1 -> x2, blocking collectives: 35.7 us -> 19.6 us  [body(): total_one, total_two = lax.psum(lax.psum((sum_one, sum_two), 'col'), 'row')]
    all_gather x1, waiting for transfers between devices: 0.02 us -> 9.15 us  [body(): piece = lax.all_gather(conv_weight, 'row', axis=3, tiled=True)]
    pmax x1, blocking collectives: 8.73 us -> 12.8 us  [body(): top = lax.pmax(raised.astype(jnp.bfloat16), 'col').astype(raised.dtype)]
  transfers between devices with their start and end apart: 7 -> 7, of which waited for: 3 -> 4; matrix products, arithmetic and copies ran while one was open for 4% -> 4% of each run, Pallas kernels for 0% -> 0%
where the time goes in v1:
time: 177 us; the launch traced here: 176 us
  blocking collectives  67.6 us (38%)
  waiting for transfers between devices  48.7 us (28%)
  matrix products  22.8 us (13%)
  between operations  14.4 us (8%)
  local copies, waits for them, and re-layouts  12.1 us (7%)
  starting transfers between devices  5.33 us (3%)
  other arithmetic  4.88 us (3%)
    reduce_scatter x1, waiting for transfers between devices, body(): lax.psum_scatter(scaled_sum.astype(jnp.bfloat16), 'col', scatter_dimensio...  23 us
    psum x2, blocking collectives, body(): total_one, total_two = lax.psum(lax.psum((sum_one, sum_two), 'col'), 'row')  19.6 us
    unnamed x4, waiting for transfers between devices  14.8 us
    all_gather x1, blocking collectives, body(): query_all = lax.all_gather(query_rows, 'col', axis=1, tiled=True)  14.6 us
    dot_general x9, matrix products, body(): jnp.dot(padded[:, down:down + rows, across:across + columns, :], piece[do...  13.7 us
    pmax x1, blocking collectives, body(): top = lax.pmax(raised.astype(jnp.bfloat16), 'col').astype(raised.dtype)  12.8 us
    all_gather x1, blocking collectives, body(): lax.all_gather(stale_k, 'row', axis=1, tiled=True)  11.6 us
    all_gather x1, waiting for transfers between devices, body(): piece = lax.all_gather(conv_weight, 'row', axis=3, tiled=True)  9.15 us
  transfers between devices with their start and end apart: 7, of which 4 were waited for; matrix products, arithmetic and copies ran while one was open for 4% of the time, Pallas kernels for 0%

profile of v1, /device:TPU:0, one launch (start us, length us, event | category | flops | bytes accessed | tf_op | source)
XLA Modules:
  0.0 176.0 jit_solution(8458504265856511704)
XLA Ops:
  8.6 13.4 %all-reduce = (f32[2,32]{1,0:T(2,128)S(1)}, f32[2,32]{1,0:T(2,128)S(1)}) all-reduce(f32[2,32]{1,0:T(2,128)S(1)} %reduce_sum.76, f32[2,32]{1,0:T(2,128)S(1)} %reduce_sum.73), channel_id=1, replica_groups=mesh['parts'=2,'row'=4,'col'=4] {'col'}, use_global_device_ids=true, to_apply=%region_6.7 | all-reduce | flops 128 | bytes 1024 | tf_op jit(solution)/shard_map/psum | solution.py:106
  22.1 6.2 %all-reduce.1 = (f32[2,32]{1,0:T(2,128)S(1)}, f32[2,32]{1,0:T(2,128)S(1)}) all-reduce(f32[2,32]{1,0:T(2,128)S(1)} %get-tuple-element.223, f32[2,32]{1,0:T(2,128)S(1)} %get-tuple-element.224), channel_id=1, replica_groups=mesh['parts'=2,'row'=4,'col'=4] {'row'}, use_global_device_ids=true, to_apply=%region_7.8 | all-reduce | flops 128 | bytes 1024 | tf_op jit(solution)/shard_map/psum | solution.py:106
  28.8 1.3 collective-permute-start
  31.7 11.6 %all_gather.13 = bf16[2,256,384]{2,0,1:T(2,128)(2,1)S(1)} all-gather(bf16[2,64,384]{2,0,1:T(2,128)(2,1)S(1)} %bitcast.148), channel_id=1, replica_groups=mesh['parts'=2,'row'=4,'col'=4] {'row'}, dimensions={1}, use_global_device_ids=true | all-gather | bytes 491520 | tf_op jit(solution)/shard_map/all_gather | solution.py:158
  43.7 9.1 %all_gather.15 = bf16[2,256,384]{2,0,1:T(2,128)(2,1)S(1)} all-gather(bf16[2,64,384]{2,0,1:T(2,128)(2,1)S(1)} %bitcast.147), channel_id=1, replica_groups=mesh['parts'=2,'row'=4,'col'=4] {'row'}, dimensions={1}, use_global_device_ids=true | all-gather | bytes 491520 | tf_op jit(solution)/shard_map/all_gather | solution.py:159
  58.3 1.8 %collective-permute-done.3 = bf16[2,10,1,640]{3,2,1,0:T(2,128)(2,1)S(1)} collective-permute-done((bf16[2,10,1,640]{3,2,1,0:T(2,128)(2,1)S(1)}, bf16[2,10,1,640]{3,2,1,0:T(2,128)(2,1)S(1)}, u32[]{:S(2)}, u32[]{:S(2)}) %collective-permute-start.3) | collective-permute-done | bytes 25632 | tf_op jit(solution)/shard_map/ppermute | solution.py:20
  60.3 9.1 %all-gather.2.cloned.1.call-done = bf16[3,3,640,640]{2,3,1,0:T(8,128)(2,1)} async-done(((bf16[3,3,640,160]{2,3,1,0:T(8,128)(2,1)}), bf16[3,3,640,640]{2,3,1,0:T(8,128)(2,1)}) %all-gather.2.cloned.1.call-update) | async-done | bytes 7372816 | tf_op jit(solution)/shard_map/all_gather | solution.py:113
  69.5 1.5 fusion.41
  71.0 1.5 fusion.38
  72.5 1.5 fusion.39
  74.0 1.5 fusion.37
  75.5 1.5 fusion.40
  77.0 1.5 fusion.35
  78.5 1.5 fusion.36
  80.1 1.5 fusion.21
  81.6 1.7 fusion.86
  87.6 14.6 %all_gather.14 = bf16[2,256,384]{2,1,0:T(8,128)(2,1)S(1)} all-gather(bf16[2,64,384]{2,1,0:T(8,128)(2,1)S(1)} %bitcast.145), channel_id=1, replica_groups=mesh['parts'=2,'row'=4,'col'=4] {'col'}, dimensions={1}, use_global_device_ids=true | all-gather | bytes 491520 | tf_op jit(solution)/shard_map/all_gather | solution.py:145
  102.3 8.8 %while.17 = (s32[]{:T(128)}, f32[2,6,256]{2,1,0:T(8,128)S(1)}, f32[2,6,256]{2,1,0:T(8,128)S(1)}, f32[2,6,256,64]{2,3,1,0:T(8,128)S(1)}, s32[]{:T(128)}, /*index=...) while((s32[]{:T(128)}, f32[2,6,256]{2,1,0:T(8,128)S(1)}, ...), condition=%wide.region_13.14_spmd.clone, body=%wide.region_10.13_spmd.clone.sunk | while | flops 104451456 | bytes 8988089 | solution.py:73
  103.8 1.4 fusion.108
  108.2 1.4 fusion.108
  112.7 12.8 %pmax.7 = bf16[2,6,256]{2,1,0:T(8,128)(2,1)S(1)} all-reduce(bf16[2,6,256]{2,1,0:T(8,128)(2,1)S(1)} %convert_element_type.78), channel_id=1, replica_groups=mesh['parts'=2,'row'=4,'col'=4] {'col'}, use_global_device_ids=true, to_apply=%region_15.16 | all-reduce | flops 3072 | bytes 12288 | tf_op jit(solution)/shard_map/pmax | solution.py:167
  127.0 1.4 multiply_convert_fusion
  129.0 14.0 %reduce-scatter.7.cloned.1.call-done = bf16[64,12]{1,0:T(8,128)(2,1)} async-done(((bf16[256,12]{1,0:T(8,128)(2,1)}), bf16[64,12]{1,0:T(8,128)(2,1)}) %reduce-scatter.7.cloned.1.call-update) | async-done | bytes 1552
  144.0 23.0 %reduce-scatter.5.cloned.1.call-done = bf16[2,6,64,64]{3,2,1,0:T(8,128)(2,1)} async-done(((bf16[2,6,256,64]{3,2,1,0:T(8,128)(2,1)}), bf16[2,6,64,64]{3,2,1,0:T(8,128)(2,1)}) %reduce-scatter.5.cloned.1.call-update) | async-done | bytes 98320 | tf_op jit(solution)/shard_map/reduce_scatter | solution.py:172
  (126 shorter events, 26.7 us)
Async XLA Ops:
  7.2 161.4 %copy-start = (bf16[384,640]{1,0:T(8,128)(2,1)S(1)}, bf16[384,640]{1,0:T(8,128)(2,1)}, u32[]{:S(2)}) copy-start(bf16[384,640]{1,0:T(8,128)(2,1)} %param.27) | copy-start | bytes 1474564
  7.2 1.0 copy-start.4
  7.2 21.4 %copy-start.13 = (f32[640]{0:T(1024)S(1)}, f32[640]{0:T(1024)}, u32[]{:S(2)}) copy-start(f32[640]{0:T(1024)} %param.18) | copy-start | bytes 7684
  7.2 21.4 %copy-start.12 = (f32[640]{0:T(1024)S(1)}, f32[640]{0:T(1024)}, u32[]{:S(2)}) copy-start(f32[640]{0:T(1024)} %param.19) | copy-start | bytes 7684
  7.2 24.2 %copy-start.16 = (s32[2]{0:T(128)S(1)}, s32[2]{0:T(128)}, u32[]{:S(2)}) copy-start(s32[2]{0:T(128)} %param.17) | copy-start | bytes 28
  7.2 24.2 %copy-start.10 = (bf16[2,8,8,384]{3,2,1,0:T(8,128)(2,1)S(1)}, bf16[2,8,8,384]{3,2,1,0:T(8,128)(2,1)}, u32[]{:S(2)}) copy-start(bf16[2,8,8,384]{3,2,1,0:T(8,128)(2,1)} %param.28) | copy-start | bytes 294916
  7.2 24.3 %copy-start.11 = (bf16[2,8,8,384]{3,2,1,0:T(8,128)(2,1)S(1)}, bf16[2,8,8,384]{3,2,1,0:T(8,128)(2,1)}, u32[]{:S(2)}) copy-start(bf16[2,8,8,384]{3,2,1,0:T(8,128)(2,1)} %param.29) | copy-start | bytes 294916
  7.2 36.2 %copy-start.7 = (bf16[320,640]{1,0:T(8,128)(2,1)S(1)}, bf16[320,640]{1,0:T(8,128)(2,1)}, u32[]{:S(2)}) copy-start(bf16[320,640]{1,0:T(8,128)(2,1)} %param.22) | copy-start | bytes 1228804
  7.3 62.2 %all-gather.2.cloned.1.call-start = ((), (), s32[]{:S(2)}) async-start(), calls=%async_computation.2 | async-start | bytes 9216000 | tf_op jit(solution)/shard_map/all_gather | solution.py:113
  8.0 135.1 %reduce-scatter.7.cloned.1.call-start = ((), (), s32[]{:S(2)}) async-start(), calls=%async_computation.4 | async-start | bytes 81920
  28.8 24.0 %collective-permute-start = (bf16[2,1,8,640]{3,2,1,0:T(8,128)(2,1)S(1)}, bf16[2,1,8,640]{3,2,1,0:T(8,128)(2,1)S(1)}, u32[]{:S(2)}, u32[]{:S(2)}) collective-permute-start(bf16[2,1,8,640]{3,2,1,0:T(8,128)(2,1)S(1)} %get-tuple-element.237), channel_id=1, source_target_pairs={{0,4},{4,8},{8,12},{1,5},{5,9},{9,13},{2,6},{6,10},{10,14},{3,7},{... | collective-permute-start | bytes 61448 | tf_op jit(solution)/shard_map/ppermute | solution.py:18
  30.1 22.6 %collective-permute-start.1 = (bf16[2,1,8,640]{3,2,1,0:T(8,128)(2,1)S(1)}, bf16[2,1,8,640]{3,2,1,0:T(8,128)(2,1)S(1)}, u32[]{:S(2)}, u32[]{:S(2)}) collective-permute-start(bf16[2,1,8,640]{3,2,1,0:T(8,128)(2,1)S(1)} %get-tuple-element.238), channel_id=1, source_target_pairs={{4,0},{8,4},{12,8},{5,1},{9,5},{13,9},{6,2},{10,6},{14,10},{7,3},{... | collective-permute-start | bytes 61448 | tf_op jit(solution)/shard_map/ppermute | solution.py:20
  52.8 5.5 %collective-permute-start.2 = (bf16[2,10,1,640]{3,2,1,0:T(2,128)(2,1)S(1)}, bf16[2,10,1,640]{3,2,1,0:T(2,128)(2,1)S(1)}, u32[]{:S(2)}, u32[]{:S(2)}) collective-permute-start(bf16[2,10,1,640]{3,2,1,0:T(2,128)(2,1)S(1)} %get-tuple-element.235), channel_id=1, source_target_pairs={{0,1},{1,2},{2,3},{4,5},{5,6},{6,7},{8,9},{9,10},{10,11},{12,13},{... | collective-permute-start | bytes 76808 | tf_op jit(solution)/shard_map/ppermute | solution.py:18
  54.1 6.0 %collective-permute-start.3 = (bf16[2,10,1,640]{3,2,1,0:T(2,128)(2,1)S(1)}, bf16[2,10,1,640]{3,2,1,0:T(2,128)(2,1)S(1)}, u32[]{:S(2)}, u32[]{:S(2)}) collective-permute-start(bf16[2,10,1,640]{3,2,1,0:T(2,128)(2,1)S(1)} %get-tuple-element.236), channel_id=1, source_target_pairs={{1,0},{2,1},{3,2},{5,4},{6,5},{7,6},{9,8},{10,9},{11,10},{13,12},{... | collective-permute-start | bytes 76808 | tf_op jit(solution)/shard_map/ppermute | solution.py:20
  80.0 1.5 copy-start.14
  81.6 1.9 %copy-start.15 = (f32[640]{0:T(1024)S(1)}, f32[640]{0:T(1024)}, u32[]{:S(2)}) copy-start(f32[640]{0:T(1024)} %param.23) | copy-start | bytes 7684
  81.6 2.0 %copy-start.5 = (bf16[640,384]{1,0:T(8,128)(2,1)S(1)}, bf16[640,384]{1,0:T(8,128)(2,1)}, u32[]{:S(2)}) copy-start(bf16[640,384]{1,0:T(8,128)(2,1)} %param.25) | copy-start | bytes 1474564
  83.3 18.9 %copy-start.1 = (f32[2,8,8,640]{3,2,1,0:T(8,128)}, f32[2,8,8,640]{3,2,1,0:T(8,128)S(1)}, u32[]{:S(2)}) copy-start(f32[2,8,8,640]{3,2,1,0:T(8,128)S(1)} %get-tuple-element.244) | copy-start | bytes 983044
  105.2 1.0 copy-start.3
  109.6 1.0 copy-start.3
  126.5 40.5 %reduce-scatter.5.cloned.1.call-start = ((), (), s32[]{:S(2)}) async-start(), calls=%async_computation.3 | async-start | bytes 983040 | tf_op jit(solution)/shard_map/reduce_scatter | solution.py:172
  127.0 1.4 copy-start.6
  128.7 39.7 %copy-start.9 = (bf16[2,8,8,384]{3,2,1,0:T(8,128)(2,1)}, bf16[2,8,8,384]{3,2,1,0:T(8,128)(2,1)S(1)}, u32[]{:S(2)}) copy-start(bf16[2,8,8,384]{3,2,1,0:T(8,128)(2,1)S(1)} %convolution_convert_fusion) | copy-start | bytes 294916
  129.0 39.5 %copy-start.2 = (f32[2,8,8,640]{3,2,1,0:T(8,128)S(1)}, f32[2,8,8,640]{3,2,1,0:T(8,128)}, u32[]{:S(2)}) copy-start(f32[2,8,8,640]{3,2,1,0:T(8,128)} %copy-done.1) | copy-start | bytes 983044
  (1 other events, 0.6 us)
Sparse Core Ops, SparseCore 0:
  9.6 59.7 all-gather.1
  126.6 16.4 reduce-scatter.6
  145.5 21.4 reduce-scatter.4
